TPU v7x, 256 devices: a whole 4x4x8 slice. The times are simulated.
256 devices in a mesh: row: 32 (over x, z), period: 8 (over y, core).
Axes of the slice: x: 4, y: 4, z: 8, core: 2. Of those that a mesh axis runs over, the one named last changes fastest.
Arguments:
- codes: int32 [8192, 64], P('row'), may hold values from 0 to 255
- node: int32 [8192], P('row'), may hold values from 0 to 15
- chosen: int32 [16, 32], replicated, may hold values from 0 to 63, all different within a row
- arm: int32 [8192], P('row'), may hold values 0 or 1
- honest: int32 [8192], P('row'), may hold values 0 or 1
- outcome: bfloat16 [8192, 128], P('row', 'period'), may hold values from -8 to 8
Outputs:
- gains: float32 [32, 16, 256], P('row', None, 'period')
- best_gain: float32 [16], replicated
- effect: float32 [16, 128], P(None, 'period')
Inputs may be any that keep to these rules, and one draw needn't show every extreme that they name: Each row of chosen holds 32 different covariate ids.
All inputs are finite; a program needn't handle non-finite values. No bound on the sum of `arm` or of `honest` on one device may be relied on, other than what follows from the above.
Results may differ from a plain program's by a relative error of at most 0.001.
Values may be sent and summed in bfloat16 or wider, within the bound.
A program may use at most 64 MiB of HBM per device.

v0:
```python
import jax
import jax.numpy as jnp
from jax import lax
from jax.sharding import PartitionSpec as P

NODES = 16
BINS = 256


def split_gain(left_sums, right_sums, weeks):

    def effect_of(sums):
        treated = sums[..., :weeks] / (sums[..., 2 * weeks : 2 * weeks + 1] + 1.0)
        control = sums[..., weeks : 2 * weeks] / (sums[..., 2 * weeks + 1 : 2 * weeks + 2] + 1.0)
        return treated - control

    spread_gap = effect_of(left_sums) - effect_of(right_sums)
    left_n = left_sums[..., 2 * weeks] + left_sums[..., 2 * weeks + 1]
    right_n = right_sums[..., 2 * weeks] + right_sums[..., 2 * weeks + 1]
    balance = left_n * right_n / ((left_n + right_n + 1.0) * (left_n + right_n + 1.0))
    return balance * jnp.sum(spread_gap * spread_gap, axis=-1)


def spread_nodes(stat_block, node_ids):
    node_hot = (node_ids[:, None] == jnp.arange(NODES, dtype=jnp.int32)[None, :]).astype(
        jnp.bfloat16
    )
    widened = node_hot[:, :, None] * stat_block[:, None, :]
    return widened.reshape(stat_block.shape[0], NODES * stat_block.shape[1])


def slot_hist(bin_column, widened):
    bin_hot = (bin_column[:, None] == jnp.arange(BINS, dtype=jnp.int32)[None, :]).astype(
        jnp.bfloat16
    )
    return lax.dot_general(
        bin_hot, widened, (((0,), (0,)), ((), ())), preferred_element_type=jnp.float32
    )


def shards(codes, node, chosen, arm, honest, outcome):
    weeks_here = outcome.shape[1]
    stat_width = 2 * weeks_here + 2
    per_owner = chosen.shape[1] // lax.axis_size("row")
    outcome_f = outcome.astype(jnp.float32)
    arm_f = arm.astype(jnp.float32)
    honest_f = honest.astype(jnp.float32)
    treated = honest_f * arm_f
    control = honest_f * (1.0 - arm_f)
    stat_cols = jnp.concatenate(
        [
            outcome_f * treated[:, None],
            outcome_f * control[:, None],
            treated[:, None],
            control[:, None],
        ],
        axis=1,
    ).astype(jnp.bfloat16)
    picked = jnp.take_along_axis(codes, chosen[node], axis=1)
    widened = spread_nodes(stat_cols, node)
    owned = lax.psum_scatter(
        lax.map(lambda column: slot_hist(column, widened), picked.T).astype(jnp.bfloat16),
        "row",
        scatter_dimension=0,
        tiled=True,
    ).astype(jnp.float32)
    hist = owned.reshape(per_owner, BINS, NODES, stat_width)
    left_sums = jnp.cumsum(hist, axis=1)
    right_sums = left_sums[:, -1:] - left_sums
    week_part = jnp.transpose(split_gain(left_sums, right_sums, weeks_here), (0, 2, 1))
    full_gain = lax.psum(week_part, "period")
    share_len = BINS // lax.axis_size("period")
    gains = lax.dynamic_slice_in_dim(full_gain, lax.axis_index("period") * share_len, share_len, 2)
    best_gain = lax.pmax(jnp.max(full_gain, axis=(0, 2)), "row")
    kept = 1.0 - honest_f
    node_hot = (node[:, None] == jnp.arange(NODES, dtype=jnp.int32)[None, :]).astype(jnp.float32)
    est_cols = jnp.concatenate(
        [outcome_f * (kept * arm_f)[:, None], outcome_f * (kept * (1.0 - arm_f))[:, None]], axis=1
    )
    est_sums = jnp.dot(node_hot.T, est_cols, precision=lax.Precision.HIGHEST)
    est_counts = jnp.dot(
        node_hot.T,
        jnp.stack([kept * arm_f, kept * (1.0 - arm_f)], axis=1),
        precision=lax.Precision.HIGHEST,
    )
    est_sums, est_counts = lax.psum((est_sums, est_counts), "row")
    effect = est_sums[:, :weeks_here] / (est_counts[:, 0:1] + 1.0) - est_sums[:, weeks_here:] / (
        est_counts[:, 1:2] + 1.0
    )
    return (gains, best_gain, effect)


def solution(mesh):
    in_specs = (P("row", None), P("row"), P(), P("row"), P("row"), P("row", "period"))
    out_specs = (P("row", None, "period"), P(), P(None, "period"))
    return jax.shard_map(shards, mesh=mesh, in_specs=in_specs, out_specs=out_specs, check_vma=False)
```

profile of v0, /device:TPU:0, one launch (start us, length us, event | category | flops | bytes accessed | tf_op | source)
XLA Modules:
  0.0 476.2 jit_solution(1574079994199093550)
XLA Ops:
  7.2 0.7 compare_select_fusion.2
  7.9 0.7 fusion.18
  8.6 0.7 convert_multiply_fusion.4
  9.3 1.4 gather_fusion
  10.8 0.1 reshape.234
  10.9 65.5 %gather_fusion.1 = s32[8192]{0:T(1024)S(1)} fusion(s32[256,64]{0,1:T(8,128)S(1)} %copy-done, s32[8192]{0:T(1024)S(1)} %reshape.234), kind=kCustom, calls=%fused_computation.1 | custom fusion | bytes 131072 | tf_op jit(solution)/shard_map/jit(take_along_axis)/gather | solution.py:59
  76.7 36.9 %while.11 = (s32[]{:T(128)}, bf16[32,256,544]{1,2,0:T(8,128)(2,1)}, s32[32,256]{1,0:T(8,128)S(1)}, bf16[256,34]{0,1:T(8,128)(2,1)S(1)}, bf16[256,16]{0,1:T(8,128)(2,1)S(1)}, /*index=5*/s32[]{:T(128)}) while((s32[]{:T(128)}, bf16[32,256,544]{1,2,0:T(8,128)(2,1)}, s32[32,256]{1,0:T(8,128)S(1)}, bf16[256,34]{0,1:T(8,128)(2,1)S(1)}, ...), condition=%wide.region_1.2_spmd.clone, body=%wide.region_0.0_spmd.clone.sunk | while | flops 71507968 | bytes 1699925 | solution.py:62
  76.8 0.1 mul.183
  76.8 1.0 fusion.32
  78.0 1.0 fusion.32
  79.1 1.0 fusion.32
  80.3 1.0 fusion.32
  81.4 1.0 fusion.32
  82.6 1.0 fusion.32
  83.6 0.1 mul.183
  83.7 1.0 fusion.32
  84.8 0.1 mul.183
  84.9 1.0 fusion.32
  86.0 1.0 fusion.32
  87.2 1.0 fusion.32
  88.3 1.0 fusion.32
  89.5 1.0 fusion.32
  90.6 1.0 fusion.32
  91.8 1.0 fusion.32
  93.0 1.1 fusion.32
  94.1 1.0 fusion.32
  95.3 1.0 fusion.32
  96.4 1.0 fusion.32
  97.6 1.0 fusion.32
  98.7 1.0 fusion.32
  99.9 1.0 fusion.32
  101.0 1.0 fusion.32
  102.2 1.0 fusion.32
  103.3 1.0 fusion.32
  104.5 1.0 fusion.32
  105.6 1.0 fusion.32
  106.8 1.0 fusion.32
  107.9 1.0 fusion.32
  109.1 1.0 fusion.32
  110.2 1.0 fusion.32
  111.4 1.0 fusion.32
  112.6 1.0 fusion.32
  113.6 0.6 copy-done.1
  114.3 0.1 fusion.17
  114.4 0.1 fusion.8
  114.5 78.8 %all-reduce = (f32[16,32]{1,0:T(8,128)S(1)}, f32[16,2]{0,1:T(2,128)S(1)}) all-reduce(f32[16,32]{1,0:T(8,128)S(1)} %fusion.8, f32[16,2]{0,1:T(2,128)S(1)} %fusion.17), channel_id=1, replica_groups=mesh['row'=32,'period'=8] {'row'}, use_global_device_ids=true, to_apply=%region_9.10 | all-reduce | flops 544 | bytes 4352 | tf_op jit(solution)/shard_map/psum | solution.py:86
  193.3 0.7 fusion.19
  194.0 151.6 %reduce-scatter.2.cloned.1.call-done = bf16[1,256,544]{1,2,0:T(8,128)(2,1)} async-done(((bf16[32,256,544]{1,2,0:T(8,128)(2,1)}), bf16[1,256,544]{1,2,0:T(8,128)(2,1)}) %reduce-scatter.2.cloned.1.call-update) | async-done | bytes 278544 | tf_op jit(solution)/shard_map/reduce_scatter | solution.py:61
  345.7 1.5 reshape.225
  347.2 19.3 %reduce-window.6 = f32[1,34,16,2,128]{4,2,3,1,0:T(8,128)S(1)} reduce-window(f32[1,34,16,2,128]{4,2,3,1,0:T(8,128)S(1)} %copy.15, f32[]{:T(128)} %constant.18.clone.1), window={size=1x1x1x1x128 pad=0_0x0_0x0_0x0_0x127_0}, to_apply=%region_3.4 | reduce-window | flops 17686528 | bytes 1114116 | tf_op jit(solution)/shard_map/reduce-window
  366.5 0.2 slice.68
  366.7 0.3 copy.16
  367.0 0.4 copy.17
  367.5 0.2 copy.18
  367.8 0.6 broadcast.82
  368.4 0.6 add_bitcast_fusion
  369.1 0.6 slice.72
  369.7 0.3 copy.24
  370.0 0.8 broadcast_subtract_fusion
  370.8 0.9 multiply_reduce_fusion
  371.9 23.6 %psum.21 = f32[1,16,256]{2,0,1:T(1,128)S(1)} all-reduce(f32[1,16,256]{2,0,1:T(1,128)S(1)} %fusion.14), channel_id=1, replica_groups=mesh['row'=32,'period'=8] {'period'}, use_global_device_ids=true, to_apply=%region_6.7 | all-reduce | flops 4096 | bytes 32768 | tf_op jit(solution)/shard_map/psum | solution.py:71
  395.4 0.2 reduce_max.9
  395.6 0.7 constant_dynamic-slice_fusion.1
  396.3 73.0 %pmax.7 = f32[16]{0:T(128)} all-reduce(f32[16]{0:T(128)S(1)} %reduce_max.9), channel_id=1, replica_groups=mesh['row'=32,'period'=8] {'row'}, use_global_device_ids=true, to_apply=%region_8.9 | all-reduce | flops 16 | bytes 128 | tf_op jit(solution)/shard_map/pmax | solution.py:74
  (119 shorter events, 4.0 us)
Async XLA Ops:
  7.2 3.7 copy-start
  7.2 338.5 %reduce-scatter.2.cloned.1.call-start = ((), (), s32[]{:S(2)}) async-start(), calls=%async_computation.1 | async-start | bytes 9191424 | tf_op jit(solution)/shard_map/reduce_scatter | solution.py:61
  10.9 65.8 %copy-start.2 = (bf16[256,16]{0,1:T(8,128)(2,1)S(1)}, bf16[256,16]{0,1:T(8,128)(2,1)}, u32[]{:S(2)}) copy-start(bf16[256,16]{0,1:T(8,128)(2,1)} %param.13) | copy-start | bytes 24580
  113.6 0.7 copy-start.1
Sparse Core Ops, SparseCore 0:
  113.8 231.8 reduce-scatter.1
where the time goes:
time: 477 us; the launch traced here: 476 us
  blocking collectives  175 us (37%)
  waiting for transfers between devices  152 us (32%)
  local copies, waits for them, and re-layouts  75.7 us (16%)
  matrix products  33.1 us (7%)
  other arithmetic  25.7 us (5%)
  between operations  14.2 us (3%)
    reduce_scatter x1, waiting for transfers between devices, shards(): lax.psum_scatter(lax.map(lambda column: slot_hist(column, widened), picke...  152 us
    psum x1, blocking collectives, shards(): est_sums, est_counts = lax.psum((est_sums, est_counts), 'row')  78.8 us
    pmax x1, blocking collectives, shards(): best_gain = lax.pmax(jnp.max(full_gain, axis=(0, 2)), 'row')  73 us
    gather x4, local copies, waits for them, and re-layouts, shards(): picked = jnp.take_along_axis(codes, chosen[node], axis=1)  67.1 us
    dot_general x32, matrix products, slot_hist(): lax.dot_general(bin_hot, widened, (((0,), (0,)), ((), ())), preferred_ele...  32.9 us
    psum x1, blocking collectives, shards(): full_gain = lax.psum(week_part, 'period')  23.6 us
    another operation x3, other arithmetic  19.9 us
  transfers between devices with their start and end apart: 1, of which 1 were waited for; matrix products, arithmetic and copies ran while one was open for 0% of the time, Pallas kernels for 0%

commit v1 on v0

v1 whole, which is shorter than its diff:
```python
import jax
import jax.numpy as jnp
from jax import lax
from jax.experimental import pallas as pl
from jax.experimental.pallas import tpu as pltpu
from jax.sharding import PartitionSpec as P

NODES = 16
SLOTS = 32
COVARS = 64
BINS = 256
NX = 4
NZ = 8
NROW = NX * NZ
NPER = 8
UNITS = 256
WEEKS = 16
MESH = pl.DeviceIdType.MESH
F32 = jnp.float32
BF16 = jnp.bfloat16


def row_peer(me, step):
    group, dx = step // NX, step % NX
    dz = ((group + 1) // 2) * (2 * (group % 2) - 1)
    x, z = me // NZ, me % NZ
    return ((x + dx) % NX) * NZ + (z + dz + NZ) % NZ


def kernel(
    codes_ref,
    node_ref,
    chosen_ref,
    arm_ref,
    honest_ref,
    outcome_ref,
    gains_ref,
    best_ref,
    effect_ref,
    obuf,
    mbuf,
    msend,
    left,
    est,
    parts,
    tops,
    o_send,
    o_recv,
    m_send,
    m_recv,
    p_send,
    p_recv,
    t_send,
    t_recv,
):
    me = lax.axis_index("row")
    per = lax.axis_index("period")

    barrier = pltpu.get_barrier_semaphore()

    def greet(step, carry):
        pl.semaphore_signal(
            barrier, inc=1, device_id={"row": row_peer(me, step)}, device_id_type=MESH
        )
        return carry

    lax.fori_loop(1, NROW, greet, 0)

    def greet_period(step, carry):
        pl.semaphore_signal(
            barrier, inc=1, device_id={"period": (per + step) % NPER}, device_id_type=MESH
        )
        return carry

    lax.fori_loop(1, NPER, greet_period, 0)

    node_row = node_ref[...].astype(F32)
    chosen_t = chosen_ref[...].astype(F32).T
    covar = lax.broadcasted_iota(jnp.int32, (SLOTS, COVARS), 1).astype(F32)
    picks = jnp.concatenate(
        [(chosen_t[:, n : n + 1] == covar).astype(F32) for n in range(NODES)], axis=0
    ).astype(BF16)
    by_node = jnp.dot(picks, codes_ref[...].astype(F32).astype(BF16), preferred_element_type=F32)
    picked = jnp.zeros((SLOTS, UNITS), F32)
    for n in range(NODES):
        picked = jnp.where(node_row == n, by_node[n * SLOTS : (n + 1) * SLOTS], picked)
    meta = jnp.concatenate(
        [node_row, arm_ref[...].astype(F32), honest_ref[...].astype(F32)], axis=0
    )
    for s in range(SLOTS):
        msend[s] = jnp.concatenate([picked[s : s + 1], meta], axis=0).astype(BF16)
    obuf[me] = outcome_ref[...]
    mbuf[me] = msend[me]

    pl.semaphore_wait(barrier, NROW - 1 + NPER - 1)

    def outcome_copy(peer, slot):
        return pltpu.make_async_remote_copy(
            src_ref=outcome_ref,
            dst_ref=obuf.at[me],
            send_sem=o_send.at[slot],
            recv_sem=o_recv.at[me],
            device_id={"row": peer},
            device_id_type=MESH,
        )

    def meta_copy(peer, slot):
        return pltpu.make_async_remote_copy(
            src_ref=msend.at[peer],
            dst_ref=mbuf.at[me],
            send_sem=m_send.at[slot],
            recv_sem=m_recv.at[me],
            device_id={"row": peer},
            device_id_type=MESH,
        )

    def send_rows(step, carry):
        peer = row_peer(me, step)
        meta_copy(peer, step).start()
        outcome_copy(peer, step).start()
        return carry

    lax.fori_loop(1, NROW, send_rows, 0)

    def arrived(peer):
        pltpu.make_async_remote_copy(
            src_ref=msend.at[peer],
            dst_ref=mbuf.at[peer],
            send_sem=m_send.at[0],
            recv_sem=m_recv.at[peer],
            device_id={"row": peer},
            device_id_type=MESH,
        ).wait_recv()
        pltpu.make_async_remote_copy(
            src_ref=outcome_ref,
            dst_ref=obuf.at[peer],
            send_sem=o_send.at[0],
            recv_sem=o_recv.at[peer],
            device_id={"row": peer},
            device_id_type=MESH,
        ).wait_recv()

    span = NX * UNITS
    bin_of = lax.broadcasted_iota(jnp.int32, (BINS, span), 0).astype(F32)
    node_of = lax.broadcasted_iota(jnp.int32, (NODES, span), 0).astype(F32)
    left[...] = jnp.zeros_like(left)
    est[...] = jnp.zeros_like(est)

    def one_hot(hit):
        return jnp.where(hit, 1.0, 0.0)

    def gather_group(group, carry):
        rows, metas = [], []
        for dx in range(NX):
            peer = row_peer(me, group * NX + dx)
            if dx == 0:

                @pl.when(group > 0)
                def _():
                    arrived(peer)

            else:
                arrived(peer)
            rows.append(obuf[peer])
            metas.append(mbuf[peer].astype(F32))
        y = jnp.concatenate(rows, axis=1).astype(F32)
        info = jnp.concatenate(metas, axis=1)
        pick, node, arm, honest = (info[k : k + 1] for k in range(4))
        away = jnp.full_like(node, float(NODES))
        in_t = jnp.where((arm * honest) > 0.0, node, away)
        in_c = jnp.where(((1.0 - arm) * honest) > 0.0, node, away)
        kept_t = jnp.where((arm * (1.0 - honest)) > 0.0, node, away)
        kept_c = jnp.where(((1.0 - arm) * (1.0 - honest)) > 0.0, node, away)
        mask = one_hot(pick <= bin_of).astype(BF16)
        wide = jnp.concatenate(
            [jnp.where(in_t == n, y, 0.0).astype(BF16) for n in range(NODES)]
            + [jnp.where(in_c == n, y, 0.0).astype(BF16) for n in range(NODES)]
            + [one_hot(in_t == node_of).astype(BF16), one_hot(in_c == node_of).astype(BF16)],
            axis=0,
        )
        left[...] += lax.dot_general(
            wide, mask, (((1,), (1,)), ((), ())), preferred_element_type=F32
        )
        kept = jnp.concatenate(
            [one_hot(kept_t == node_of).astype(BF16), one_hot(kept_c == node_of).astype(BF16)],
            axis=0,
        )
        stats = jnp.concatenate([y.astype(BF16), jnp.ones((16, span), BF16)], axis=0)
        est[...] += lax.dot_general(
            kept, stats, (((1,), (1,)), ((), ())), preferred_element_type=F32
        )
        return carry

    lax.fori_loop(0, NZ, gather_group, 0)

    half = NODES * WEEKS
    count_t = left[2 * half : 2 * half + NODES, :]
    count_c = left[2 * half + NODES :, :]
    rest_t = count_t[:, BINS - 1 :] - count_t
    rest_c = count_c[:, BINS - 1 :] - count_c
    w_lt = 1.0 / (count_t + 1.0)
    w_lc = 1.0 / (count_c + 1.0)
    w_rt = 1.0 / (rest_t + 1.0)
    w_rc = 1.0 / (rest_c + 1.0)
    sums = []
    for n in range(NODES):
        lt = left[n * WEEKS : (n + 1) * WEEKS, :]
        lc = left[half + n * WEEKS : half + (n + 1) * WEEKS, :]
        rt = lt[:, BINS - 1 :] - lt
        rc = lc[:, BINS - 1 :] - lc
        gap = (lt * w_lt[n : n + 1] - lc * w_lc[n : n + 1]) - (
            rt * w_rt[n : n + 1] - rc * w_rc[n : n + 1]
        )
        sums.append(jnp.sum(gap * gap, axis=0, keepdims=True))
    parts[per] = jnp.concatenate(sums, axis=0)

    def part_copy(step):
        other = (per + step) % NPER
        return pltpu.make_async_remote_copy(
            src_ref=parts.at[per],
            dst_ref=parts.at[per],
            send_sem=p_send.at[step],
            recv_sem=p_recv.at[per],
            device_id={"period": other},
            device_id_type=MESH,
        )

    for step in range(1, NPER):
        part_copy(step).start()

    effect_ref[...] = est[:NODES, :WEEKS] / (est[:NODES, WEEKS : WEEKS + 1] + 1.0) - est[
        NODES:, :WEEKS
    ] / (est[NODES:, WEEKS : WEEKS + 1] + 1.0)
    n_l = count_t + count_c
    n_r = rest_t + rest_c
    balance = n_l * n_r / ((n_l + n_r + 1.0) * (n_l + n_r + 1.0))

    for step in range(1, NPER):
        other = (per + step) % NPER
        pltpu.make_async_remote_copy(
            src_ref=parts.at[other],
            dst_ref=parts.at[other],
            send_sem=p_send.at[step],
            recv_sem=p_recv.at[other],
            device_id={"period": other},
            device_id_type=MESH,
        ).wait_recv()
    spread = parts[0]
    for p in range(1, NPER):
        spread = spread + parts[p]
    full = balance * spread

    peak = jnp.max(full, axis=1, keepdims=True)
    diag = lax.broadcasted_iota(jnp.int32, (NODES, 128), 0) == lax.broadcasted_iota(
        jnp.int32, (NODES, 128), 1
    )
    tops[me] = jnp.sum(jnp.where(diag, peak, 0.0), axis=0, keepdims=True)

    def top_copy(peer, slot):
        return pltpu.make_async_remote_copy(
            src_ref=tops.at[me],
            dst_ref=tops.at[me],
            send_sem=t_send.at[slot],
            recv_sem=t_recv.at[me],
            device_id={"row": peer},
            device_id_type=MESH,
        )

    def send_tops(step, carry):
        top_copy(row_peer(me, step), step).start()
        return carry

    lax.fori_loop(1, NROW, send_tops, 0)

    share = BINS // NPER
    mine = jnp.zeros((NODES, share), F32)
    for p in range(NPER):
        mine = jnp.where(per == p, full[:, p * share : (p + 1) * share], mine)
    gains_ref[...] = mine

    def top_wait(step, carry):
        peer = row_peer(me, step)
        pltpu.make_async_remote_copy(
            src_ref=tops.at[peer],
            dst_ref=tops.at[peer],
            send_sem=t_send.at[step],
            recv_sem=t_recv.at[peer],
            device_id={"row": peer},
            device_id_type=MESH,
        ).wait_recv()
        return carry

    lax.fori_loop(1, NROW, top_wait, 0)
    best_ref[...] = jnp.max(tops[...], axis=0)[:, :NODES]

    def drain(step, carry):
        peer = row_peer(me, step)
        meta_copy(peer, step).wait_send()
        outcome_copy(peer, step).wait_send()
        top_copy(peer, step).wait_send()
        return carry

    lax.fori_loop(1, NROW, drain, 0)
    for step in range(1, NPER):
        part_copy(step).wait_send()


def shards(codes, node, chosen, arm, honest, outcome):
    vmem = pl.BlockSpec(memory_space=pltpu.VMEM)
    dma = pltpu.SemaphoreType.DMA
    gains, best, effect = pl.pallas_call(
        kernel,
        out_shape=(
            jax.ShapeDtypeStruct((NODES, BINS // NPER), F32),
            jax.ShapeDtypeStruct((1, NODES), F32),
            jax.ShapeDtypeStruct((NODES, WEEKS), F32),
        ),
        in_specs=[vmem] * 6,
        out_specs=(vmem,) * 3,
        scratch_shapes=[
            pltpu.VMEM((NROW, WEEKS, UNITS), BF16),
            pltpu.VMEM((NROW, 4, UNITS), BF16),
            pltpu.VMEM((NROW, 4, UNITS), BF16),
            pltpu.VMEM((2 * NODES * WEEKS + 2 * NODES, BINS), F32),
            pltpu.VMEM((2 * NODES, 32), F32),
            pltpu.VMEM((NPER, NODES, BINS), F32),
            pltpu.VMEM((NROW, 1, 128), F32),
            dma((NROW,)),
            dma((NROW,)),
            dma((NROW,)),
            dma((NROW,)),
            dma((NPER,)),
            dma((NPER,)),
            dma((NROW,)),
            dma((NROW,)),
        ],
        compiler_params=pltpu.CompilerParams(collective_id=0, has_side_effects=True),
        name="level",
    )(
        codes.T,
        node.reshape(1, UNITS),
        chosen,
        arm.reshape(1, UNITS),
        honest.reshape(1, UNITS),
        outcome.T,
    )
    return gains[None], best.reshape(NODES), effect


def solution(mesh):
    in_specs = (P("row", None), P("row"), P(), P("row"), P("row"), P("row", "period"))
    out_specs = (P("row", None, "period"), P(), P(None, "period"))
    return jax.shard_map(shards, mesh=mesh, in_specs=in_specs, out_specs=out_specs, check_vma=False)
```

time: 477 us -> 41.7 us (0.09)
  the two profiles are of different devices: /device:TPU:0 before, /device:TPU:1 now
where the time goes in v1:
time: 41.7 us; the launch traced here: 41.5 us
  Pallas kernels  38.5 us (92%)
  local copies, waits for them, and re-layouts  2.41 us (6%)
  between operations  0.65 us (2%)
    pallas_call x1, Pallas kernels, shards(): pl.pallas_call(kernel, out_shape=(jax.ShapeDtypeStruct((NODES, BINS // NP...  38.5 us
    unnamed x9, local copies, waits for them, and re-layouts  2.41 us

profile of v1, /device:TPU:1, one launch (start us, length us, event | category | flops | bytes accessed | tf_op | source)
XLA Modules:
  0.0 41.5 jit_solution(2739569227361533651)
XLA Ops:
  0.6 38.5 %level.1 = (f32[16,32]{1,0:T(8,128)}, f32[1,16]{1,0:T(1,128)}, f32[16,16]{1,0:T(8,128)}) custom-call(s32[64,256]{1,0:T(8,128)} %bitcast.7, s32[1,256]{1,0:T(1,128)} %bitcast.10, s32[16,32]{1,0:T(8,128)} %chosen_ref.1, s32[1,256]{1,0:T(1,128)} %bitcast.11, s32[1,256]{1,0:T(1,128)} %bitcast.12, bf16[16,256]{1,0:T(8,128)(2,1)} %bitcast.9), custom_call_target="tpu_custom_call" | custom-call | tf_op jit(solution)/shard_map/level/pallas_call | solution.py:311
  39.1 0.0 copy-start.1
  39.1 0.7 %copy-done.1 = f32[16,32]{1,0:T(8,128)S(1)} copy-done((f32[16,32]{1,0:T(8,128)S(1)}, f32[16,32]{1,0:T(8,128)}, u32[]{:S(2)}) %copy-start.1) | copy-done | bytes 2072
  39.8 0.0 copy-start.2
  39.8 0.0 copy-start
  39.8 0.6 %copy.12 = f32[1,16,32]{2,1,0:T(8,128)} copy(f32[1,16,32]{2,1,0:T(8,128)S(1)} %bitcast.8) | data formatting | bytes 4096
  40.4 0.0 copy-done.2
  40.4 0.5 %copy.13 = f32[16]{0:T(128)} copy(f32[16]{0:T(128)S(1)} %bitcast.13) | data formatting | bytes 128
  40.9 0.0 copy-done
  40.9 0.6 %copy.14 = f32[16,16]{1,0:T(8,128)} copy(f32[16,16]{1,0:T(8,128)S(1)} %copy-done) | data formatting | bytes 2048
Async XLA Ops:
  39.1 0.7 %copy-start.1 = (f32[16,32]{1,0:T(8,128)S(1)}, f32[16,32]{1,0:T(8,128)}, u32[]{:S(2)}) copy-start(f32[16,32]{1,0:T(8,128)} %get-tuple-element.6) | copy-start | bytes 6148
  39.8 0.6 %copy-start.2 = (f32[1,16]{1,0:T(1,128)S(1)}, f32[1,16]{1,0:T(1,128)}, u32[]{:S(2)}) copy-start(f32[1,16]{1,0:T(1,128)} %get-tuple-element.7) | copy-start | bytes 196
  39.8 1.1 %copy-start = (f32[16,16]{1,0:T(8,128)S(1)}, f32[16,16]{1,0:T(8,128)}, u32[]{:S(2)}) copy-start(f32[16,16]{1,0:T(8,128)} %get-tuple-element.14) | copy-start | bytes 3076

commit v2 on v1

v2 whole, which is shorter than its diff:
```python
import jax
import jax.numpy as jnp
from jax import lax
from jax.experimental import pallas as pl
from jax.experimental.pallas import tpu as pltpu
from jax.sharding import PartitionSpec as P

NODES = 16
SLOTS = 32
COVARS = 64
BINS = 256
NX = 4
NZ = 8
NROW = NX * NZ
NPER = 8
UNITS = 256
WEEKS = 16
HALF = NODES * WEEKS
MESH = pl.DeviceIdType.MESH
F32 = jnp.float32
BF16 = jnp.bfloat16
Z_SEND = (4, 3, -3, 2, -2, 1, -1)
Z_TAKE = (0, 1, -1, 2, -2, 3, -3, 4)
X_SEND = (2, 1, 3)
P_SEND = (4, 5, 3, 2, 6, 7, 1)


def kernel(
    codes_hbm,
    node_hbm,
    chosen_hbm,
    arm_hbm,
    honest_hbm,
    outcome_hbm,
    gains_ref,
    best_ref,
    effect_ref,
    codes_ref,
    node_ref,
    chosen_ref,
    arm_ref,
    honest_ref,
    obuf,
    msend,
    mzbuf,
    mxbuf,
    left,
    est,
    parts,
    tops,
    in_sem,
    zo_send,
    zm_send,
    xo_send,
    xm_send,
    o_recv,
    mz_recv,
    mx_recv,
    p_send,
    p_recv,
    t_send,
    t_recv,
):
    me = lax.axis_index("row")
    per = lax.axis_index("period")
    my_x = lax.div(me, NZ)
    my_z = lax.rem(me, NZ)
    z_at = {dz: lax.rem(my_z + (dz + NZ), NZ) for dz in Z_TAKE}
    x_at = {dx: lax.rem(my_x + dx, NX) for dx in range(NX)}

    def row_of(dx, dz):
        return x_at[dx] * NZ + z_at[dz]

    barrier = pltpu.get_barrier_semaphore()
    for dz in Z_SEND:
        pl.semaphore_signal(
            barrier, inc=1, device_id={"row": row_of(0, dz)}, device_id_type=MESH
        )
    for dx in X_SEND:
        pl.semaphore_signal(
            barrier, inc=1, device_id={"row": row_of(dx, 0)}, device_id_type=MESH
        )
    for dp in P_SEND:
        pl.semaphore_signal(
            barrier, inc=1, device_id={"period": lax.rem(per + dp, NPER)}, device_id_type=MESH
        )

    loads = [
        pltpu.make_async_copy(src, dst, in_sem.at[k])
        for k, (src, dst) in enumerate(
            [
                (codes_hbm, codes_ref),
                (node_hbm, node_ref),
                (chosen_hbm, chosen_ref),
                (arm_hbm, arm_ref),
                (honest_hbm, honest_ref),
                (outcome_hbm, obuf.at[me]),
            ]
        )
    ]
    for load in loads:
        load.start()
    for load in loads:
        load.wait()

    node_row = node_ref[...].astype(F32)
    chosen_t = chosen_ref[...].astype(F32).T
    covar = lax.broadcasted_iota(jnp.int32, (SLOTS, COVARS), 1).astype(F32)
    picks = jnp.concatenate(
        [jnp.where(chosen_t[:, n : n + 1] == covar, 1.0, 0.0) for n in range(NODES)], axis=0
    ).astype(BF16)
    by_node = jnp.dot(picks, codes_ref[...].astype(F32).astype(BF16), preferred_element_type=F32)
    picked = jnp.zeros((SLOTS, UNITS), F32)
    for n in range(NODES):
        picked = jnp.where(node_row == n, by_node[n * SLOTS : (n + 1) * SLOTS], picked)
    meta = jnp.concatenate(
        [node_row, arm_ref[...].astype(F32), honest_ref[...].astype(F32)], axis=0
    )
    for s in range(SLOTS):
        msend[s % NZ, s // NZ] = jnp.concatenate([picked[s : s + 1], meta], axis=0).astype(BF16)

    pl.semaphore_wait(barrier, len(Z_SEND) + len(X_SEND) + len(P_SEND))

    def outcome_to_z(dz):
        return pltpu.make_async_remote_copy(
            src_ref=obuf.at[me],
            dst_ref=obuf.at[me],
            send_sem=zo_send.at[dz % NZ],
            recv_sem=o_recv.at[me],
            device_id={"row": row_of(0, dz)},
            device_id_type=MESH,
        )

    def meta_to_z(dz):
        return pltpu.make_async_remote_copy(
            src_ref=msend.at[z_at[dz]],
            dst_ref=mzbuf.at[my_z],
            send_sem=zm_send.at[dz % NZ],
            recv_sem=mz_recv.at[my_z],
            device_id={"row": row_of(0, dz)},
            device_id_type=MESH,
        )

    def outcome_to_x(dz, dx):
        row = row_of(0, dz)
        return pltpu.make_async_remote_copy(
            src_ref=obuf.at[row],
            dst_ref=obuf.at[row],
            send_sem=xo_send.at[(dz % NZ) * NX + dx],
            recv_sem=o_recv.at[row],
            device_id={"row": row_of(dx, 0)},
            device_id_type=MESH,
        )

    def meta_to_x(dz, dx):
        row = row_of(0, dz)
        source = msend.at[my_z] if dz == 0 else mzbuf.at[z_at[dz]]
        return pltpu.make_async_remote_copy(
            src_ref=source.at[x_at[dx]],
            dst_ref=mxbuf.at[row],
            send_sem=xm_send.at[(dz % NZ) * NX + dx],
            recv_sem=mx_recv.at[row],
            device_id={"row": row_of(dx, 0)},
            device_id_type=MESH,
        )

    def outcome_arrived(row):
        pltpu.make_async_remote_copy(
            src_ref=obuf.at[row],
            dst_ref=obuf.at[row],
            send_sem=zo_send.at[0],
            recv_sem=o_recv.at[row],
            device_id={"row": row},
            device_id_type=MESH,
        ).wait_recv()

    for dz in Z_SEND:
        meta_to_z(dz).start()
        outcome_to_z(dz).start()
    for dx in X_SEND:
        meta_to_x(0, dx).start()
        outcome_to_x(0, dx).start()

    left[...] = jnp.zeros_like(left)
    mxbuf[me] = msend[my_z, my_x]
    for dz in Z_TAKE[1:]:
        row = row_of(0, dz)
        pltpu.make_async_remote_copy(
            src_ref=mzbuf.at[z_at[dz]],
            dst_ref=mzbuf.at[z_at[dz]],
            send_sem=zm_send.at[0],
            recv_sem=mz_recv.at[z_at[dz]],
            device_id={"row": row},
            device_id_type=MESH,
        ).wait_recv()
        for dx in X_SEND:
            meta_to_x(dz, dx).start()
        outcome_arrived(row)
        for dx in X_SEND:
            outcome_to_x(dz, dx).start()
        mxbuf[row] = mzbuf[z_at[dz], my_x]

    def load_rows(rows):
        y = jnp.concatenate([obuf[row] for row in rows], axis=1)
        info = jnp.concatenate([mxbuf[row].astype(F32) for row in rows], axis=1)
        return y, [info[k : k + 1] for k in range(4)]

    def spread(row):
        return jnp.broadcast_to(row, (NODES, row.shape[1])).astype(BF16)

    def add_rows(rows):
        y, (pick, node, arm, honest) = load_rows(rows)
        span = y.shape[1]
        away = jnp.full_like(node, float(NODES))
        in_t = spread(jnp.where((arm * honest) > 0.0, node, away))
        in_c = spread(jnp.where(((1.0 - arm) * honest) > 0.0, node, away))
        pick = spread(pick)
        lane = lax.broadcasted_iota(jnp.int32, (NODES, span), 0).astype(F32).astype(BF16)
        one = jnp.ones((NODES, span), BF16)
        zero = jnp.zeros((NODES, span), BF16)
        mask = jnp.concatenate(
            [
                jnp.where(pick <= lane + jnp.asarray(float(k * NODES), BF16), one, zero)
                for k in range(BINS // NODES)
            ],
            axis=0,
        )
        wide = jnp.concatenate(
            [jnp.where(in_t == jnp.asarray(float(n), BF16), y, zero) for n in range(NODES)]
            + [jnp.where(in_c == jnp.asarray(float(n), BF16), y, zero) for n in range(NODES)]
            + [jnp.where(in_t == lane, one, zero), jnp.where(in_c == lane, one, zero)],
            axis=0,
        )
        left[...] += lax.dot_general(
            wide, mask, (((1,), (1,)), ((), ())), preferred_element_type=F32
        )

    add_rows([row_of(0, dz) for dz in Z_TAKE])

    def take_pair(pair, carry):
        rows = []
        for k in range(2):
            step = pair * 2 + k
            dz = ((step + 1) // 2) * (2 * (step % 2) - 1)
            z = lax.rem(my_z + dz + NZ, NZ)
            for dx in X_SEND:
                row = x_at[dx] * NZ + z
                pltpu.make_async_remote_copy(
                    src_ref=mxbuf.at[row],
                    dst_ref=mxbuf.at[row],
                    send_sem=zm_send.at[0],
                    recv_sem=mx_recv.at[row],
                    device_id={"row": row},
                    device_id_type=MESH,
                ).wait_recv()
                outcome_arrived(row)
                rows.append(row)
        add_rows(rows)
        return carry

    lax.fori_loop(0, NZ // 2, take_pair, 0)

    count_t = left[2 * HALF : 2 * HALF + NODES, :]
    count_c = left[2 * HALF + NODES :, :]
    rest_t = count_t[:, BINS - 1 :] - count_t
    rest_c = count_c[:, BINS - 1 :] - count_c
    w_lt = 1.0 / (count_t + 1.0)
    w_lc = 1.0 / (count_c + 1.0)
    w_rt = 1.0 / (rest_t + 1.0)
    w_rc = 1.0 / (rest_c + 1.0)

    def part_copy(chunk, dp, owner):
        return pltpu.make_async_remote_copy(
            src_ref=parts.at[chunk, owner],
            dst_ref=parts.at[chunk, owner],
            send_sem=p_send.at[chunk * NPER + dp],
            recv_sem=p_recv.at[chunk * NPER + owner],
            device_id={"period": lax.rem(per + dp, NPER)},
            device_id_type=MESH,
        )

    for chunk in range(2):
        sums = []
        for n in range(chunk * 8, chunk * 8 + 8):
            lt = left[n * WEEKS : (n + 1) * WEEKS, :]
            lc = left[HALF + n * WEEKS : HALF + (n + 1) * WEEKS, :]
            rt = lt[:, BINS - 1 :] - lt
            rc = lc[:, BINS - 1 :] - lc
            gap = (lt * w_lt[n : n + 1] - lc * w_lc[n : n + 1]) - (
                rt * w_rt[n : n + 1] - rc * w_rc[n : n + 1]
            )
            sums.append(jnp.sum(gap * gap, axis=0, keepdims=True))
        parts[chunk, per] = jnp.concatenate(sums, axis=0)
        for dp in P_SEND:
            part_copy(chunk, dp, per).start()

    est[...] = jnp.zeros_like(est)

    def add_kept(z, carry):
        y, (_, node, arm, honest) = load_rows([x * NZ + z for x in range(NX)])
        span = y.shape[1]
        away = jnp.full_like(node, float(NODES))
        kept_t = spread(jnp.where((arm * (1.0 - honest)) > 0.0, node, away))
        kept_c = spread(jnp.where(((1.0 - arm) * (1.0 - honest)) > 0.0, node, away))
        lane = lax.broadcasted_iota(jnp.int32, (NODES, span), 0).astype(F32).astype(BF16)
        one = jnp.ones((NODES, span), BF16)
        zero = jnp.zeros((NODES, span), BF16)
        kept = jnp.concatenate(
            [jnp.where(kept_t == lane, one, zero), jnp.where(kept_c == lane, one, zero)], axis=0
        )
        est[...] += lax.dot_general(
            kept,
            jnp.concatenate([y, one], axis=0),
            (((1,), (1,)), ((), ())),
            preferred_element_type=F32,
        )
        return carry

    lax.fori_loop(0, NZ, add_kept, 0)
    effect_ref[...] = est[:NODES, :WEEKS] / (est[:NODES, WEEKS : WEEKS + 1] + 1.0) - est[
        NODES:, :WEEKS
    ] / (est[NODES:, WEEKS : WEEKS + 1] + 1.0)
    n_l = count_t + count_c
    n_r = rest_t + rest_c
    balance = n_l * n_r / ((n_l + n_r + 1.0) * (n_l + n_r + 1.0))

    spreads = []
    for chunk in range(2):
        for dp in P_SEND:
            part_copy(chunk, dp, lax.rem(per + dp, NPER)).wait_recv()
        total = parts[chunk, 0]
        for p in range(1, NPER):
            total = total + parts[chunk, p]
        spreads.append(total)
    full = balance * jnp.concatenate(spreads, axis=0)

    peak = jnp.max(full, axis=1, keepdims=True)
    diag = lax.broadcasted_iota(jnp.int32, (NODES, 128), 0) == lax.broadcasted_iota(
        jnp.int32, (NODES, 128), 1
    )
    tops[me] = jnp.sum(jnp.where(diag, peak, 0.0), axis=0, keepdims=True)

    far_first = sorted(
        ((dx, dz) for dx in range(NX) for dz in Z_TAKE if dx or dz),
        key=lambda d: -(min(d[0], NX - d[0]) + abs(d[1])),
    )

    def top_copy(dx, dz, owner):
        return pltpu.make_async_remote_copy(
            src_ref=tops.at[owner],
            dst_ref=tops.at[owner],
            send_sem=t_send.at[dx * NZ + dz % NZ],
            recv_sem=t_recv.at[owner],
            device_id={"row": row_of(dx, dz)},
            device_id_type=MESH,
        )

    for dx, dz in far_first:
        top_copy(dx, dz, me).start()

    share = BINS // NPER
    mine = jnp.zeros((NODES, share), F32)
    for p in range(NPER):
        mine = jnp.where(per == p, full[:, p * share : (p + 1) * share], mine)
    gains_ref[...] = mine

    for dz in Z_SEND:
        meta_to_z(dz).wait_send()
        outcome_to_z(dz).wait_send()
    for dz in Z_TAKE:
        for dx in X_SEND:
            meta_to_x(dz, dx).wait_send()
            outcome_to_x(dz, dx).wait_send()
    for chunk in range(2):
        for dp in P_SEND:
            part_copy(chunk, dp, per).wait_send()

    for dx, dz in far_first:
        top_copy(dx, dz, row_of(dx, dz)).wait_recv()
    best_ref[...] = jnp.max(tops[...], axis=0)[:, :NODES]
    for dx, dz in far_first:
        top_copy(dx, dz, me).wait_send()


def shards(codes, node, chosen, arm, honest, outcome):
    vmem = pl.BlockSpec(memory_space=pltpu.VMEM)
    hbm = pl.BlockSpec(memory_space=pl.ANY)
    dma = pltpu.SemaphoreType.DMA
    gains, best, effect = pl.pallas_call(
        kernel,
        out_shape=(
            jax.ShapeDtypeStruct((NODES, BINS // NPER), F32),
            jax.ShapeDtypeStruct((1, NODES), F32),
            jax.ShapeDtypeStruct((NODES, WEEKS), F32),
        ),
        in_specs=[hbm] * 6,
        out_specs=(vmem,) * 3,
        scratch_shapes=[
            pltpu.VMEM((COVARS, UNITS), jnp.int32),
            pltpu.VMEM((1, UNITS), jnp.int32),
            pltpu.VMEM((NODES, SLOTS), jnp.int32),
            pltpu.VMEM((1, UNITS), jnp.int32),
            pltpu.VMEM((1, UNITS), jnp.int32),
            pltpu.VMEM((NROW, WEEKS, UNITS), BF16),
            pltpu.VMEM((NZ, NX, 4, UNITS), BF16),
            pltpu.VMEM((NZ, NX, 4, UNITS), BF16),
            pltpu.VMEM((NROW, 4, UNITS), BF16),
            pltpu.VMEM((2 * HALF + 2 * NODES, BINS), F32),
            pltpu.VMEM((2 * NODES, 2 * WEEKS), F32),
            pltpu.VMEM((2, NPER, 8, BINS), F32),
            pltpu.VMEM((NROW, 1, 128), F32),
            dma((6,)),
            dma((NZ,)),
            dma((NZ,)),
            dma((NROW,)),
            dma((NROW,)),
            dma((NROW,)),
            dma((NZ,)),
            dma((NROW,)),
            dma((2 * NPER,)),
            dma((2 * NPER,)),
            dma((NROW,)),
            dma((NROW,)),
        ],
        compiler_params=pltpu.CompilerParams(collective_id=0, has_side_effects=True),
        name="level",
    )(
        codes.T,
        node.reshape(1, UNITS),
        chosen,
        arm.reshape(1, UNITS),
        honest.reshape(1, UNITS),
        outcome.T,
    )
    return gains[None], best.reshape(NODES), effect


def solution(mesh):
    in_specs = (P("row", None), P("row"), P(), P("row"), P("row"), P("row", "period"))
    out_specs = (P("row", None, "period"), P(), P(None, "period"))
    return jax.shard_map(shards, mesh=mesh, in_specs=in_specs, out_specs=out_specs, check_vma=False)
```

time: 41.7 us -> 36.2 us (0.87)
  Pallas kernels: 38.5 us -> 32.9 us
    pallas_call x1, Pallas kernels: 38.5 us -> 32.9 us  [shards(): pl.pallas_call(kernel, out_shape=(jax.ShapeDtypeStruct((NODES, BINS // NP...]
where the time goes in v2:
time: 36.2 us; the launch traced here: 36 us
  Pallas kernels  32.9 us (91%)
  local copies, waits for them, and re-layouts  2.41 us (7%)
  between operations  0.65 us (2%)
    pallas_call x1, Pallas kernels, shards(): pl.pallas_call(kernel, out_shape=(jax.ShapeDtypeStruct((NODES, BINS // NP...  32.9 us
    unnamed x9, local copies, waits for them, and re-layouts  2.41 us

profile of v2, /device:TPU:1, one launch (start us, length us, event | category | flops | bytes accessed | tf_op | source)
XLA Modules:
  0.0 36.0 jit_solution(9550930620342350522)
XLA Ops:
  0.6 32.9 %level.1 = (f32[16,32]{1,0:T(8,128)}, f32[1,16]{1,0:T(1,128)}, f32[16,16]{1,0:T(8,128)}) custom-call(s32[64,256]{1,0:T(8,128)} %bitcast.7, s32[1,256]{1,0:T(1,128)} %bitcast.10, s32[16,32]{1,0:T(8,128)} %chosen_hbm.1, s32[1,256]{1,0:T(1,128)} %bitcast.11, s32[1,256]{1,0:T(1,128)} %bitcast.12, bf16[16,256]{1,0:T(8,128)(2,1)} %bitcast.9), custom_call_target="tpu_custom_call" | custom-call | tf_op jit(solution)/shard_map/level/pallas_call | solution.py:389
  33.5 0.0 copy-start.1
  33.6 0.7 %copy-done.1 = f32[16,32]{1,0:T(8,128)S(1)} copy-done((f32[16,32]{1,0:T(8,128)S(1)}, f32[16,32]{1,0:T(8,128)}, u32[]{:S(2)}) %copy-start.1) | copy-done | bytes 2072
  34.2 0.0 copy-start.2
  34.2 0.0 copy-start
  34.2 0.6 %copy.12 = f32[1,16,32]{2,1,0:T(8,128)} copy(f32[1,16,32]{2,1,0:T(8,128)S(1)} %bitcast.8) | data formatting | bytes 4096
  34.8 0.0 copy-done.2
  34.8 0.5 %copy.13 = f32[16]{0:T(128)} copy(f32[16]{0:T(128)S(1)} %bitcast.13) | data formatting | bytes 128
  35.4 0.0 copy-done
  35.4 0.6 %copy.14 = f32[16,16]{1,0:T(8,128)} copy(f32[16,16]{1,0:T(8,128)S(1)} %copy-done) | data formatting | bytes 2048
Async XLA Ops:
  33.5 0.7 %copy-start.1 = (f32[16,32]{1,0:T(8,128)S(1)}, f32[16,32]{1,0:T(8,128)}, u32[]{:S(2)}) copy-start(f32[16,32]{1,0:T(8,128)} %get-tuple-element.6) | copy-start | bytes 6148
  34.2 0.6 %copy-start.2 = (f32[1,16]{1,0:T(1,128)S(1)}, f32[1,16]{1,0:T(1,128)}, u32[]{:S(2)}) copy-start(f32[1,16]{1,0:T(1,128)} %get-tuple-element.7) | copy-start | bytes 196
  34.2 1.1 %copy-start = (f32[16,16]{1,0:T(8,128)S(1)}, f32[16,16]{1,0:T(8,128)}, u32[]{:S(2)}) copy-start(f32[16,16]{1,0:T(8,128)} %get-tuple-element.14) | copy-start | bytes 3076

commit v3 on v2

--- a/solution.py
+++ b/solution.py
@@ -32,9 +32,7 @@
     arm_hbm,
     honest_hbm,
     outcome_hbm,
-    gains_ref,
-    best_ref,
-    effect_ref,
+    packed_ref,
     codes_ref,
     node_ref,
     chosen_ref,
@@ -182,6 +180,7 @@
         outcome_to_x(0, dx).start()
 
     left[...] = jnp.zeros_like(left)
+    packed_ref[...] = jnp.zeros_like(packed_ref)
     mxbuf[me] = msend[my_z, my_x]
     for dz in Z_TAKE[1:]:
         row = row_of(0, dz)
@@ -317,7 +316,7 @@
         return carry
 
     lax.fori_loop(0, NZ, add_kept, 0)
-    effect_ref[...] = est[:NODES, :WEEKS] / (est[:NODES, WEEKS : WEEKS + 1] + 1.0) - est[
+    packed_ref[NODES : 2 * NODES, :WEEKS] = est[:NODES, :WEEKS] / (est[:NODES, WEEKS : WEEKS + 1] + 1.0) - est[
         NODES:, :WEEKS
     ] / (est[NODES:, WEEKS : WEEKS + 1] + 1.0)
     n_l = count_t + count_c
@@ -362,7 +361,7 @@
     mine = jnp.zeros((NODES, share), F32)
     for p in range(NPER):
         mine = jnp.where(per == p, full[:, p * share : (p + 1) * share], mine)
-    gains_ref[...] = mine
+    packed_ref[:NODES, :share] = mine
 
     for dz in Z_SEND:
         meta_to_z(dz).wait_send()
@@ -377,24 +376,26 @@
 
     for dx, dz in far_first:
         top_copy(dx, dz, row_of(dx, dz)).wait_recv()
-    best_ref[...] = jnp.max(tops[...], axis=0)[:, :NODES]
+    packed_ref[2 * NODES : 2 * NODES + 1, :] = jnp.max(tops[...], axis=0)
     for dx, dz in far_first:
         top_copy(dx, dz, me).wait_send()
+
+
+def split_results(packed_ref, gains_ref, best_ref, effect_ref):
+    gains_ref[...] = packed_ref[:NODES, : BINS // NPER]
+    best_ref[...] = packed_ref[2 * NODES : 2 * NODES + 1, :NODES]
+    effect_ref[...] = packed_ref[NODES : 2 * NODES, :WEEKS]
 
 
 def shards(codes, node, chosen, arm, honest, outcome):
     vmem = pl.BlockSpec(memory_space=pltpu.VMEM)
     hbm = pl.BlockSpec(memory_space=pl.ANY)
     dma = pltpu.SemaphoreType.DMA
-    gains, best, effect = pl.pallas_call(
+    packed = pl.pallas_call(
         kernel,
-        out_shape=(
-            jax.ShapeDtypeStruct((NODES, BINS // NPER), F32),
-            jax.ShapeDtypeStruct((1, NODES), F32),
-            jax.ShapeDtypeStruct((NODES, WEEKS), F32),
-        ),
+        out_shape=jax.ShapeDtypeStruct((2 * NODES + 8, 128), F32),
         in_specs=[hbm] * 6,
-        out_specs=(vmem,) * 3,
+        out_specs=vmem,
         scratch_shapes=[
             pltpu.VMEM((COVARS, UNITS), jnp.int32),
             pltpu.VMEM((1, UNITS), jnp.int32),
@@ -432,6 +433,17 @@
         honest.reshape(1, UNITS),
         outcome.T,
     )
+    gains, best, effect = pl.pallas_call(
+        split_results,
+        out_shape=(
+            jax.ShapeDtypeStruct((NODES, BINS // NPER), F32),
+            jax.ShapeDtypeStruct((1, NODES), F32),
+            jax.ShapeDtypeStruct((NODES, WEEKS), F32),
+        ),
+        in_specs=[vmem],
+        out_specs=(vmem,) * 3,
+        name="split_results",
+    )(packed)
     return gains[None], best.reshape(NODES), effect
 
 

time: 36.2 us -> 35.1 us (0.970)
  local copies, waits for them, and re-layouts: 2.41 us -> 0 us
  Pallas kernels: 32.9 us -> 34.2 us
    unnamed x9 -> x0, local copies, waits for them, and re-layouts: 2.41 us -> none
    pallas_call x1 -> x2, Pallas kernels: 32.9 us -> 34.2 us  [the longest x1 32.9 us: shards(): pl.pallas_call(kernel, out_shape=jax.ShapeDtypeStruct((2 * NODES + 8, 128...]
where the time goes in v3:
time: 35.1 us; the launch traced here: 34.9 us
  Pallas kernels  34.2 us (97%)
  between operations  0.64 us (2%)
    pallas_call x1, Pallas kernels, shards(): pl.pallas_call(kernel, out_shape=jax.ShapeDtypeStruct((2 * NODES + 8, 128...  32.9 us
    pallas_call x1, Pallas kernels, shards(): pl.pallas_call(split_results, out_shape=(jax.ShapeDtypeStruct((NODES, BIN...  1.34 us

profile of v3, /device:TPU:1, one launch (start us, length us, event | category | flops | bytes accessed | tf_op | source)
XLA Modules:
  0.0 34.9 jit_solution(8754596069746839652)
XLA Ops:
  0.6 32.9 %level.1.packed_ref = f32[40,128]{1,0:T(8,128)} custom-call(s32[64,256]{1,0:T(8,128)} %bitcast.7, s32[1,256]{1,0:T(1,128)} %bitcast.9, s32[16,32]{1,0:T(8,128)} %chosen_hbm.1, s32[1,256]{1,0:T(1,128)} %bitcast.10, s32[1,256]{1,0:T(1,128)} %bitcast.11, bf16[16,256]{1,0:T(8,128)(2,1)} %bitcast.8), custom_call_target="tpu_custom_call" | custom-call | tf_op jit(solution)/shard_map/level/pallas_call | solution.py:394
  33.5 1.3 %split_results.1 = (f32[16,32]{1,0:T(8,128)}, f32[1,16]{1,0:T(1,128)}, f32[16,16]{1,0:T(8,128)}) custom-call(f32[40,128]{1,0:T(8,128)} %level.1.packed_ref), custom_call_target="tpu_custom_call" | custom-call | tf_op jit(solution)/shard_map/split_results/pallas_call | solution.py:436

commit v4 on v3

--- a/solution.py
+++ b/solution.py
@@ -393,7 +393,7 @@
     dma = pltpu.SemaphoreType.DMA
     packed = pl.pallas_call(
         kernel,
-        out_shape=jax.ShapeDtypeStruct((2 * NODES + 8, 128), F32),
+        out_shape=pltpu.VMEM((2 * NODES + 8, 128), F32),
         in_specs=[hbm] * 6,
         out_specs=vmem,
         scratch_shapes=[
@@ -443,7 +443,7 @@
         in_specs=[vmem],
         out_specs=(vmem,) * 3,
         name="split_results",
-    )(packed)
+    )(pltpu.with_memory_space_constraint(packed, pltpu.VMEM))
     return gains[None], best.reshape(NODES), effect
 
 

time: 35.1 us -> 33.7 us (0.960)
  Pallas kernels: 34.2 us -> 32.9 us
    pallas_call x1, Pallas kernels: 1.34 us -> 0.61 us  [shards(): pl.pallas_call(split_results, out_shape=(jax.ShapeDtypeStruct((NODES, BIN...]
    pallas_call x1, Pallas kernels: 32.9 us -> 32.3 us  [shards(): pl.pallas_call(kernel, out_shape=pltpu.VMEM((2 * NODES + 8, 128), F32), i...]
where the time goes in v4:
time: 33.7 us; the launch traced here: 33.5 us
  Pallas kernels  32.9 us (98%)
  between operations  0.64 us (2%)
    pallas_call x1, Pallas kernels, shards(): pl.pallas_call(kernel, out_shape=pltpu.VMEM((2 * NODES + 8, 128), F32), i...  32.3 us

profile of v4, /device:TPU:1, one launch (start us, length us, event | category | flops | bytes accessed | tf_op | source)
XLA Modules:
  0.0 33.5 jit_solution(15696764826452875073)
XLA Ops:
  0.6 32.3 %level.1.packed_ref = f32[40,128]{1,0:T(8,128)S(1)} custom-call(s32[64,256]{1,0:T(8,128)} %bitcast.7, s32[1,256]{1,0:T(1,128)} %bitcast.9, s32[16,32]{1,0:T(8,128)} %chosen_hbm.1, s32[1,256]{1,0:T(1,128)} %bitcast.10, s32[1,256]{1,0:T(1,128)} %bitcast.11, bf16[16,256]{1,0:T(8,128)(2,1)} %bitcast.8), custom_call_target="tpu_custom_call" | custom-call | tf_op jit(solution)/shard_map/level/pallas_call | solution.py:394
  32.9 0.6 %split_results.1 = (f32[16,32]{1,0:T(8,128)}, f32[1,16]{1,0:T(1,128)}, f32[16,16]{1,0:T(8,128)}) custom-call(f32[40,128]{1,0:T(8,128)S(1)} %level.1.packed_ref), custom_call_target="tpu_custom_call" | custom-call | tf_op jit(solution)/shard_map/split_results/pallas_call | solution.py:436

commit v5 on v4

--- a/solution.py
+++ b/solution.py
@@ -69,20 +69,6 @@
     def row_of(dx, dz):
         return x_at[dx] * NZ + z_at[dz]
 
-    barrier = pltpu.get_barrier_semaphore()
-    for dz in Z_SEND:
-        pl.semaphore_signal(
-            barrier, inc=1, device_id={"row": row_of(0, dz)}, device_id_type=MESH
-        )
-    for dx in X_SEND:
-        pl.semaphore_signal(
-            barrier, inc=1, device_id={"row": row_of(dx, 0)}, device_id_type=MESH
-        )
-    for dp in P_SEND:
-        pl.semaphore_signal(
-            barrier, inc=1, device_id={"period": lax.rem(per + dp, NPER)}, device_id_type=MESH
-        )
-
     loads = [
         pltpu.make_async_copy(src, dst, in_sem.at[k])
         for k, (src, dst) in enumerate(
@@ -98,6 +84,20 @@
     ]
     for load in loads:
         load.start()
+    barrier = pltpu.get_barrier_semaphore()
+    for dz in Z_SEND:
+        pl.semaphore_signal(
+            barrier, inc=1, device_id={"row": row_of(0, dz)}, device_id_type=MESH
+        )
+    for dx in X_SEND:
+        pl.semaphore_signal(
+            barrier, inc=1, device_id={"row": row_of(dx, 0)}, device_id_type=MESH
+        )
+    for dp in P_SEND:
+        pl.semaphore_signal(
+            barrier, inc=1, device_id={"period": lax.rem(per + dp, NPER)}, device_id_type=MESH
+        )
+
     for load in loads:
         load.wait()
 

time: 33.7 us -> 33.7 us (level)
  no operation moved by 1% of the time
where the time goes in v5:
time: 33.7 us; the launch traced here: 33.6 us
  Pallas kernels  32.9 us (98%)
  between operations  0.64 us (2%)
    pallas_call x1, Pallas kernels, shards(): pl.pallas_call(kernel, out_shape=pltpu.VMEM((2 * NODES + 8, 128), F32), i...  32.3 us

profile of v5, /device:TPU:1, one launch (start us, length us, event | category | flops | bytes accessed | tf_op | source)
XLA Modules:
  0.0 33.6 jit_solution(11349591076094769512)
XLA Ops:
  0.6 32.3 %level.1.packed_ref = f32[40,128]{1,0:T(8,128)S(1)} custom-call(s32[64,256]{1,0:T(8,128)} %bitcast.7, s32[1,256]{1,0:T(1,128)} %bitcast.9, s32[16,32]{1,0:T(8,128)} %chosen_hbm.1, s32[1,256]{1,0:T(1,128)} %bitcast.10, s32[1,256]{1,0:T(1,128)} %bitcast.11, bf16[16,256]{1,0:T(8,128)(2,1)} %bitcast.8), custom_call_target="tpu_custom_call" | custom-call | tf_op jit(solution)/shard_map/level/pallas_call | solution.py:394
  32.9 0.6 %split_results.1 = (f32[16,32]{1,0:T(8,128)}, f32[1,16]{1,0:T(1,128)}, f32[16,16]{1,0:T(8,128)}) custom-call(f32[40,128]{1,0:T(8,128)S(1)} %level.1.packed_ref), custom_call_target="tpu_custom_call" | custom-call | tf_op jit(solution)/shard_map/split_results/pallas_call | solution.py:436
